TPU v7x, 256 devices: a whole 4x4x8 slice. The times are simulated.
256 devices in a mesh: rep: 16 (over y_lo, z), tp: 16 (over x, y_hi, core).
Axes of the slice: x: 4, y: 4 (y_hi: 2, y_lo: 2; y = y_hi * 2 + y_lo), z: 8, core: 2. Of those that a mesh axis runs over, the one named last changes fastest.
Arguments:
- tokens: bfloat16 [16384, 8192], P('rep', 'tp'), may hold values from -6 to 6
- grad_out: bfloat16 [16384, 4096], P('rep', 'tp'), may hold values from -0.046875 to 0.046875
- lengths: int32 [16, 16], replicated, may hold values from 0 to 256, as said below
- master: float32 [8192, 2048], P('rep', 'tp'), may hold values from -3 to 3
- first: float32 [8192, 2048], P('rep', 'tp'), may hold values from -6 to 6
- second: float32 [8192, 2048], P('rep', 'tp'), may hold values from 0.25 to 4
Outputs:
- new_master: float32 [8192, 2048], P('rep', 'tp')
- new_first: float32 [8192, 2048], P('rep', 'tp')
- new_second: float32 [8192, 2048], P('rep', 'tp')
- healthy_weights: bfloat16 [8192, 2048], P(None, 'tp')
- slot_weights: bfloat16 [16, 8192, 4096], P('rep', None, 'tp')
Inputs may be any that keep to these rules, and one draw needn't show every extreme that they name: `lengths`: each row is one replica's split of the 2048 columns over its devices in tp order: the entries are multiples of 64, sum to 2048, the nonzero ones come first and number at least half of the row; a row is either all 128 or has an entry equal to 256, and some row has an entry equal to 256.
All inputs are finite; a program needn't handle non-finite values.
Results may differ from a plain program's by a relative error of at most 0.0019.
Values may be sent and summed in bfloat16 or wider, within the bound.
No kernel may reach another device: no remote copies, remote signals or barrier semaphores. Data moves between devices by JAX's collectives and lax.ppermute only.
A program may use at most 128 MiB of HBM per device.

v0:
```python
import jax
import jax.numpy as jnp
from jax import lax
from jax.sharding import Mesh
from jax.sharding import PartitionSpec as P

COLS = 2048
STEP = 1000
REP = ("rep_0", "rep_1")
decay_first = 0.9
decay_second = 0.999
learning_rate = 0.02
weight_decay = 0.1
epsilon = 1e-08


def own_block(parts, axes, turns):
    inside = parts.shape[1:]
    parts = parts.reshape(*(lax.axis_size(a) for a in axes), *inside)
    parts = jnp.moveaxis(parts, turns, range(len(axes))).reshape(-1, *inside)
    for k in turns:
        parts = lax.psum_scatter(parts, axes[k], scatter_dimension=0, tiled=True)
    return parts[0]


def in_blocks(value, dim, size):
    before, after = (value.shape[:dim], value.shape[dim + 1 :])
    return jnp.moveaxis(value.reshape(*before, size, -1, *after), dim, 0)


def summed_rows(value, axes, turns, dim):
    size = lax.axis_size(axes)
    return own_block(in_blocks(value, dim, size), axes, turns)


def from_everyone(value, axis):
    copies = jnp.broadcast_to(value, (lax.axis_size(axis), *value.shape))
    return lax.all_to_all(copies, axis, split_axis=0, concat_axis=0, tiled=True)


def laid_out(parts, dim):
    shape = list(parts.shape[1:])
    shape[dim] *= parts.shape[0]
    return jnp.moveaxis(parts, 0, dim).reshape(shape)


def gathered_copies(value, axis, dim):
    parts = from_everyone(value, axis)
    return laid_out(parts, dim)


def adam_update(master, first, second, gradient):
    scale_first = 1.0 - decay_first**STEP
    scale_second = 1.0 - decay_second**STEP
    new_first = decay_first * first + (1.0 - decay_first) * gradient
    new_second = decay_second * second + (1.0 - decay_second) * gradient * gradient
    direction = new_first / scale_first / (jnp.sqrt(new_second / scale_second) + epsilon)
    new_master = master - learning_rate * (direction + weight_decay * master)
    return (new_master, new_first, new_second)


def on_device(tokens, grad_out, lengths, master, first, second):
    shards = lax.axis_size("tp")
    replicas = lax.axis_size(REP)
    column_index = lax.axis_index("tp")
    replica_index = lax.axis_index(REP)
    token_count = tokens.shape[0]
    slot_width = grad_out.shape[1]
    block_width = COLS // shards
    begins_all = jnp.cumsum(lengths, axis=1) - lengths
    is_mine = jnp.arange(shards, dtype=jnp.int32) == column_index
    own_lengths = lax.dynamic_index_in_dim(lengths, replica_index, 0, keepdims=False)
    own_begins = lax.dynamic_index_in_dim(begins_all, replica_index, 0, keepdims=False)
    my_begin = jnp.sum(jnp.where(is_mine, own_begins, 0))
    my_length = jnp.sum(jnp.where(is_mine, own_lengths, 0))
    columns = jnp.arange(COLS, dtype=jnp.int32)
    offset = columns - my_begin
    inside = (offset >= 0) & (offset < my_length)
    picked = jnp.take(grad_out, jnp.clip(offset, 0, slot_width - 1), axis=1)
    spread = jnp.where(inside[None, :], picked, jnp.zeros_like(picked)).reshape(
        token_count, shards, block_width
    )
    received = lax.all_to_all(spread, "tp", split_axis=1, concat_axis=1, tiled=True)
    grad_block = jnp.sum(received, axis=1)
    grad_columns = lax.dot_general(
        lax.all_gather(tokens, "tp", axis=1, tiled=True),
        grad_block,
        (((0,), (0,)), ((), ())),
        preferred_element_type=jnp.float32,
    )
    summed = summed_rows(grad_columns.astype(jnp.bfloat16), REP, (1, 0), 0).astype(jnp.float32)
    new_master, new_first, new_second = adam_update(master, first, second, summed)
    weights = new_master.astype(jnp.bfloat16)
    healthy = gathered_copies(weights, REP, 0)
    replica_rows = lax.all_gather(weights, "tp", axis=1, tiled=True)
    slot_begins = jnp.sum(jnp.where(is_mine[None, :], begins_all, 0), axis=1)
    slot_lengths = jnp.sum(jnp.where(is_mine[None, :], lengths, 0), axis=1)
    within = jnp.arange(slot_width, dtype=jnp.int32)
    source_cols = slot_begins[:, None] + within[None, :]
    valid = within[None, :] < slot_lengths[:, None]
    taken = jnp.take(replica_rows, jnp.clip(source_cols, 0, COLS - 1).reshape(-1), axis=1)
    outgoing = jnp.where(valid.reshape(-1)[None, :], taken, jnp.zeros_like(taken))
    outgoing = outgoing.reshape(replica_rows.shape[0], replicas, slot_width)
    arrived = lax.all_to_all(outgoing, REP, split_axis=1, concat_axis=0, tiled=True)
    slot_weights = arrived.reshape(1, -1, slot_width)
    return (new_master, new_first, new_second, healthy, slot_weights)


def solution(mesh):
    torus = Mesh(mesh.devices.reshape(2, 8, mesh.shape["tp"]), ("rep_0", "rep_1", "tp"))
    placed = (P(REP, "tp"), P(REP, "tp"), P(), P(REP, "tp"), P(REP, "tp"), P(REP, "tp"))
    return jax.shard_map(
        on_device,
        mesh=torus,
        in_specs=placed,
        out_specs=(P(REP, "tp"), P(REP, "tp"), P(REP, "tp"), P(None, "tp"), P(REP, None, "tp")),
        check_vma=False,
    )
```

profile of v0, /device:TPU:32, one launch (start us, length us, event | category | flops | bytes accessed | tf_op | source)
XLA Modules:
  0.0 450.8 jit_solution(10688095374911271748)
XLA Ops:
  7.2 0.0 all-gather.3.cloned.1.call-start
  7.2 0.7 all-gather.3.cloned.1.call-update
  7.9 0.0 reduce-scatter.3.cloned.1.call-start
  8.0 0.9 reduce_window_sum.11
  8.8 1.2 copy.34
  10.1 0.8 select_reduce_fusion.1
  10.9 1.3 fusion.12
  12.2 0.7 compare_select_fusion.1
  12.9 9.6 %gather_fusion = bf16[2048,1024]{1,0:T(8,128)(2,1)} fusion(bf16[1024,256]{0,1:T(8,128)(2,1)S(1)} %copy.34, s32[2048]{0:T(1024)S(1)} %broadcast_clamp_fusion.1), kind=kCustom, calls=%fused_computation | custom fusion | bytes 8396800 | tf_op jit(solution)/shard_map/jit(_take)/gather | solution.py:79
  22.5 0.7 fusion.10
  23.2 1.3 fusion.11
  24.5 3.1 select_select_fusion.1
  27.6 73.9 %all_to_all.25 = bf16[1024,16,128]{0,2,1:T(8,128)(2,1)} all-to-all(bf16[1024,16,128]{0,2,1:T(8,128)(2,1)S(1)} %select_select_fusion.1), channel_id=1, replica_groups=mesh['rep_0'=2,'rep_1'=8,'tp'=16] {'tp'}, dimensions={1} | all-to-all | bytes 8388608 | tf_op jit(solution)/shard_map/all_to_all | solution.py:83
  101.5 3.1 reduce_sum.50
  104.7 63.9 %all-gather.3.cloned.1.call-done = bf16[1024,8192]{1,0:T(8,128)(2,1)} async-done(((bf16[1024,512]{1,0:T(8,128)(2,1)}), bf16[1024,8192]{1,0:T(8,128)(2,1)}) %all-gather.3.cloned.1.call-update) | async-done | bytes 16777232 | tf_op jit(solution)/shard_map/all_gather | solution.py:86
  168.6 8.1 %convolution_convert_fusion = bf16[128,8192]{1,0:T(8,128)(2,1)S(1)} fusion(bf16[1024,128]{0,1:T(8,128)(2,1)S(1)} %reduce_sum.50, bf16[1024,8192]{1,0:T(8,128)(2,1)} %all-gather.3.cloned.1.call-done), kind=kOutput, calls=%fused_computation.2 | convolution fusion | flops 2148532224 | bytes 19136512 | tf_op jit(solution)/shard_map/dot_general | solution.py:85
  176.7 0.9 copy.44
  177.6 0.0 copy-start
  177.6 0.0 copy-start.1
  177.6 0.0 copy-start.2
  177.6 2.5 copy.35
  180.1 0.0 reduce-scatter.3.cloned.1.call-update
  180.1 0.0 reduce-scatter.5.cloned.1.call-start
  180.2 41.0 %reduce-scatter.3.cloned.1.call-done = bf16[2,512,128]{1,2,0:T(8,128)(2,1)} async-done(((bf16[16,512,128]{1,2,0:T(8,128)(2,1)}), bf16[2,512,128]{1,2,0:T(8,128)(2,1)}) %reduce-scatter.3.cloned.1.call-update) | async-done | bytes 262160 | tf_op jit(solution)/shard_map/reduce_scatter | solution.py:22
  221.2 0.0 reduce-scatter.5.cloned.1.call-update
  221.2 0.0 all-gather.5.cloned.1.call-start
  221.2 0.1 copy.33
  221.4 0.1 copy.36
  221.5 0.1 copy.38
  221.7 18.0 %reduce-scatter.5.cloned.1.call-done = bf16[1,512,128]{1,2,0:T(8,128)(2,1)} async-done(((bf16[2,512,128]{1,2,0:T(8,128)(2,1)}), bf16[1,512,128]{1,2,0:T(8,128)(2,1)}) %reduce-scatter.5.cloned.1.call-update) | async-done | bytes 131088 | tf_op jit(solution)/shard_map/reduce_scatter | solution.py:22
  239.7 1.8 fusion.14
  241.5 0.0 all-gather.5.cloned.1.call-update
  241.5 1.0 copy.39
  242.5 1.7 broadcast_in_dim.78
  244.3 7.5 %all-to-all-start.1 = ((bf16[16,512,128]{2,1,0:T(8,128)(2,1)}), bf16[16,512,128]{2,1,0:T(8,128)(2,1)S(1)}, u32[]{:S(2)}, u32[]{:S(2)}) async-start(bf16[16,512,128]{2,1,0:T(8,128)(2,1)} %broadcast_in_dim.78), calls=%async_computation.3 | async-start | bytes 4194304 | tf_op jit(solution)/shard_map/all_to_all | solution.py:38
  251.8 0.1 fusion.2
  251.9 0.1 iota_compare_fusion
  252.0 52.9 %all-gather.5.cloned.1.call-done = bf16[512,2048]{0,1:T(8,128)(2,1)} async-done(((bf16[512,128]{0,1:T(8,128)(2,1)}), bf16[512,2048]{0,1:T(8,128)(2,1)}) %all-gather.5.cloned.1.call-update) | async-done | bytes 2097168 | tf_op jit(solution)/shard_map/all_gather | solution.py:95
  304.9 19.3 %gather_fusion.1 = bf16[4096,512]{1,0:T(8,128)(2,1)} fusion(bf16[512,2048]{0,1:T(8,128)(2,1)} %all-gather.5.cloned.1.call-done, s32[4096]{0:T(1024)S(1)} %broadcast_clamp_fusion), kind=kCustom, calls=%fused_computation.1 | custom fusion | bytes 8404992 | tf_op jit(solution)/shard_map/jit(_take)/gather | solution.py:101
  324.2 5.2 %select_select_fusion = bf16[512,16,256]{0,2,1:T(8,128)(2,1)} fusion(bf16[512,16,256]{0,2,1:T(8,128)(2,1)} %bitcast.43, pred[16,256]{1,0:T(8,128)(4,1)S(1)} %get-tuple-element.30, pred[16,256]{1,0:T(8,128)(4,1)S(1)} %get-tuple-element.29), kind=kLoop, calls=%fused_computation.3 | loop fusion | flops 4194304 | bytes 8396800 | tf_op jit(solution)/shard_map/jit(_where)/select_n | solution.py:102
  329.5 0.0 all-to-all-done.1
  329.5 11.3 %all-to-all-start.2 = ((bf16[512,16,256]{0,2,1:T(8,128)(2,1)}), bf16[512,16,256]{0,2,1:T(8,128)(2,1)}, u32[]{:S(2)}, u32[]{:S(2)}) async-start(bf16[512,16,256]{0,2,1:T(8,128)(2,1)} %select_select_fusion), calls=%async_computation.4 | async-start | bytes 8388608 | tf_op jit(solution)/shard_map/all_to_all | solution.py:104
  340.7 0.8 copy.41
  341.6 0.8 copy.42
  342.4 0.8 copy.43
  343.2 93.3 %all-to-all-done.2 = bf16[512,16,256]{0,2,1:T(8,128)(2,1)} async-done(((bf16[512,16,256]{0,2,1:T(8,128)(2,1)}), bf16[512,16,256]{0,2,1:T(8,128)(2,1)}, u32[]{:S(2)}, u32[]{:S(2)}) %all-to-all-start.2) | async-done | bytes 4194336 | tf_op jit(solution)/shard_map/all_to_all | solution.py:104
  436.6 6.4 %copy.40 = bf16[16,512,1,256]{3,1,0,2:T(8,128)(2,1)} copy(bf16[16,512,1,256]{1,3,0,2:T(8,128)(2,1)} %bitcast.15) | data formatting | bytes 8388608 | tf_op jit(solution)/shard_map/all_to_all | solution.py:104
  443.0 1.3 copy.47
  (8 shorter events, 0.1 us)
Async XLA Ops:
  7.2 161.4 %all-gather.3.cloned.1.call-start = ((), (), s32[]{:S(2)}) async-start(), calls=%async_computation.5 | async-start | bytes 17825792 | tf_op jit(solution)/shard_map/all_gather | solution.py:86
  7.9 213.3 %reduce-scatter.3.cloned.1.call-start = ((), (), s32[]{:S(2)}) async-start(), calls=%async_computation.6 | async-start | bytes 2359296 | tf_op jit(solution)/shard_map/reduce_scatter | solution.py:22
  177.6 43.7 %copy-start = (f32[512,128]{1,0:T(8,128)S(1)}, f32[512,128]{1,0:T(8,128)}, u32[]{:S(2)}) copy-start(f32[512,128]{1,0:T(8,128)} %param.10) | copy-start | bytes 786436
  177.6 43.8 %copy-start.1 = (f32[512,128]{1,0:T(8,128)S(1)}, f32[512,128]{1,0:T(8,128)}, u32[]{:S(2)}) copy-start(f32[512,128]{1,0:T(8,128)} %param.11) | copy-start | bytes 786436
  177.6 43.9 %copy-start.2 = (f32[512,128]{1,0:T(8,128)S(1)}, f32[512,128]{1,0:T(8,128)}, u32[]{:S(2)}) copy-start(f32[512,128]{1,0:T(8,128)} %param.9) | copy-start | bytes 786436
  180.1 59.6 %reduce-scatter.5.cloned.1.call-start = ((), (), s32[]{:S(2)}) async-start(), calls=%async_computation.7 | async-start | bytes 393216 | tf_op jit(solution)/shard_map/reduce_scatter | solution.py:22
  221.2 83.7 %all-gather.5.cloned.1.call-start = ((), (), s32[]{:S(2)}) async-start(), calls=%async_computation.8 | async-start | bytes 2228224 | tf_op jit(solution)/shard_map/all_gather | solution.py:95
  244.3 85.2 %all-to-all-start.1 = ((bf16[16,512,128]{2,1,0:T(8,128)(2,1)}), bf16[16,512,128]{2,1,0:T(8,128)(2,1)S(1)}, u32[]{:S(2)}, u32[]{:S(2)}) async-start(bf16[16,512,128]{2,1,0:T(8,128)(2,1)} %broadcast_in_dim.78), calls=%async_computation.3 | async-start | bytes 4194304 | tf_op jit(solution)/shard_map/all_to_all | solution.py:38
  329.5 107.1 %all-to-all-start.2 = ((bf16[512,16,256]{0,2,1:T(8,128)(2,1)}), bf16[512,16,256]{0,2,1:T(8,128)(2,1)}, u32[]{:S(2)}, u32[]{:S(2)}) async-start(bf16[512,16,256]{0,2,1:T(8,128)(2,1)} %select_select_fusion), calls=%async_computation.4 | async-start | bytes 8388608 | tf_op jit(solution)/shard_map/all_to_all | solution.py:104
Sparse Core Ops, SparseCore 0:
  10.5 158.0 all-gather.2
  180.3 40.8 reduce-scatter.2
  223.7 16.0 reduce-scatter.4
  242.8 62.0 all-gather.4
where the time goes:
time: 452 us; the launch traced here: 451 us
  waiting for transfers between devices  270 us (60%)
  blocking collectives  73.9 us (16%)
  local copies, waits for them, and re-layouts  46.9 us (10%)
  other arithmetic  19.1 us (4%)
  starting transfers between devices  18.9 us (4%)
  between operations  13.9 us (3%)
  matrix products  8.12 us (2%)
    all_to_all x1, waiting for transfers between devices, on_device(): lax.all_to_all(outgoing, REP, split_axis=1, concat_axis=0, tiled=True)  93.3 us
    all_to_all x1, blocking collectives, on_device(): lax.all_to_all(spread, 'tp', split_axis=1, concat_axis=1, tiled=True)  73.9 us
    all_gather x1, waiting for transfers between devices, on_device(): lax.all_gather(tokens, 'tp', axis=1, tiled=True)  63.9 us
    reduce_scatter x2, waiting for transfers between devices, own_block(): parts = lax.psum_scatter(parts, axes[k], scatter_dimension=0, tiled=True)  59 us
    all_gather x1, waiting for transfers between devices, on_device(): replica_rows = lax.all_gather(weights, 'tp', axis=1, tiled=True)  52.9 us
    gather x1, local copies, waits for them, and re-layouts, on_device(): jnp.take(replica_rows, jnp.clip(source_cols, 0, COLS - 1).reshape(-1), ax...  19.3 us
    all_to_all x1, starting transfers between devices, on_device(): lax.all_to_all(outgoing, REP, split_axis=1, concat_axis=0, tiled=True)  11.3 us
    gather x1, local copies, waits for them, and re-layouts, on_device(): picked = jnp.take(grad_out, jnp.clip(offset, 0, slot_width - 1), axis=1)  9.61 us
  transfers between devices with their start and end apart: 6, of which 5 were waited for; matrix products, arithmetic and copies ran while one was open for 12% of the time, Pallas kernels for 0%

commit v1 on v0

--- a/solution.py
+++ b/solution.py
@@ -83,7 +83,7 @@
     received = lax.all_to_all(spread, "tp", split_axis=1, concat_axis=1, tiled=True)
     grad_block = jnp.sum(received, axis=1)
     grad_columns = lax.dot_general(
-        lax.all_gather(tokens, "tp", axis=1, tiled=True),
+        jnp.concatenate(lax.all_gather(tokens, "tp"), axis=1),
         grad_block,
         (((0,), (0,)), ((), ())),
         preferred_element_type=jnp.float32,

time: 452 us -> 464 us (1.027)
  local copies, waits for them, and re-layouts: 46.9 us -> 68.6 us
  waiting for transfers between devices: 270 us -> 258 us
    reshape x0 -> x1, local copies, waits for them, and re-layouts: none -> 21.7 us  [on_device(): jnp.concatenate(lax.all_gather(tokens, 'tp'), axis=1)]
    all_gather x1, waiting for transfers between devices: 63.9 us -> 52.1 us  [on_device(): lax.all_gather(tokens, 'tp')]
  transfers between devices with their start and end apart: 6 -> 6, of which waited for: 5 -> 5; matrix products, arithmetic and copies ran while one was open for 12% -> 11% of each run, Pallas kernels for 0% -> 0%
where the time goes in v1:
time: 464 us; the launch traced here: 463 us
  waiting for transfers between devices  258 us (56%)
  blocking collectives  72.6 us (16%)
  local copies, waits for them, and re-layouts  68.6 us (15%)
  other arithmetic  19.1 us (4%)
  starting transfers between devices  18.9 us (4%)
  between operations  13.9 us (3%)
  matrix products  11.3 us (2%)
    all_to_all x1, waiting for transfers between devices, on_device(): lax.all_to_all(outgoing, REP, split_axis=1, concat_axis=0, tiled=True)  93.3 us
    all_to_all x1, blocking collectives, on_device(): lax.all_to_all(spread, 'tp', split_axis=1, concat_axis=1, tiled=True)  72.6 us
    reduce_scatter x2, waiting for transfers between devices, own_block(): parts = lax.psum_scatter(parts, axes[k], scatter_dimension=0, tiled=True)  59 us
    all_gather x1, waiting for transfers between devices, on_device(): replica_rows = lax.all_gather(weights, 'tp', axis=1, tiled=True)  53 us
    all_gather x1, waiting for transfers between devices, on_device(): lax.all_gather(tokens, 'tp')  52.1 us
    reshape x1, local copies, waits for them, and re-layouts, on_device(): jnp.concatenate(lax.all_gather(tokens, 'tp'), axis=1)  21.7 us
    gather x1, local copies, waits for them, and re-layouts, on_device(): jnp.take(replica_rows, jnp.clip(source_cols, 0, COLS - 1).reshape(-1), ax...  19.3 us
    dot_general x1, matrix products, on_device(): lax.dot_general(jnp.concatenate(lax.all_gather(tokens, 'tp'), axis=1), gr...  11.3 us
  transfers between devices with their start and end apart: 6, of which 5 were waited for; matrix products, arithmetic and copies ran while one was open for 11% of the time, Pallas kernels for 0%

profile of v1, /device:TPU:32, one launch (start us, length us, event | category | flops | bytes accessed | tf_op | source)
XLA Modules:
  0.0 462.5 jit_solution(2251249999387566332)
XLA Ops:
  7.2 0.0 all-gather.6.cloned.1.call-start
  7.2 0.7 all-gather.6.cloned.1.call-update
  7.9 0.0 reduce-scatter.3.cloned.1.call-start
  8.0 0.9 reduce_window_sum.11
  8.8 1.2 copy.46
  10.1 0.8 select_reduce_fusion.1
  10.9 1.3 fusion.12
  12.2 0.7 compare_select_fusion.1
  12.9 9.6 %gather_fusion = bf16[2048,1024]{1,0:T(8,128)(2,1)} fusion(bf16[1024,256]{0,1:T(8,128)(2,1)S(1)} %copy.46, s32[2048]{0:T(1024)S(1)} %broadcast_clamp_fusion.1), kind=kCustom, calls=%fused_computation | custom fusion | bytes 8396800 | tf_op jit(solution)/shard_map/jit(_take)/gather | solution.py:79
  22.5 0.7 fusion.10
  23.2 1.3 fusion.11
  24.5 3.1 select_select_fusion.1
  27.6 72.6 %all_to_all.25 = bf16[1024,16,128]{0,2,1:T(8,128)(2,1)} all-to-all(bf16[1024,16,128]{0,2,1:T(8,128)(2,1)S(1)} %select_select_fusion.1), channel_id=1, replica_groups=mesh['rep_0'=2,'rep_1'=8,'tp'=16] {'tp'}, dimensions={1} | all-to-all | bytes 8388608 | tf_op jit(solution)/shard_map/all_to_all | solution.py:83
  100.2 3.1 reduce_sum.50
  103.3 52.1 %all-gather.6.cloned.1.call-done = bf16[16384,512]{1,0:T(8,128)(2,1)} async-done(((bf16[1024,512]{1,0:T(8,128)(2,1)}), bf16[16384,512]{1,0:T(8,128)(2,1)}) %all-gather.6.cloned.1.call-update) | async-done | bytes 16777232 | tf_op jit(solution)/shard_map/all_gather | solution.py:86
  155.4 21.7 %copy.47 = bf16[1024,16,512]{0,2,1:T(8,128)(2,1)} copy(bf16[1024,16,512]{2,0,1:T(8,128)(2,1)} %bitcast.50) | data formatting | bytes 33554432 | tf_op jit(solution)/shard_map/reshape | solution.py:86
  177.1 11.3 %convolution_convert_fusion = bf16[128,8192]{1,0:T(8,128)(2,1)S(1)} fusion(bf16[1024,128]{0,1:T(8,128)(2,1)S(1)} %reduce_sum.50, bf16[1024,8192]{0,1:T(8,128)(2,1)} %bitcast.47), kind=kOutput, calls=%fused_computation.2 | convolution fusion | flops 2148532224 | bytes 19136512 | tf_op jit(solution)/shard_map/dot_general | solution.py:85
  188.5 0.8 copy.57
  189.3 0.0 copy-start
  189.3 0.0 copy-start.1
  189.3 0.0 copy-start.2
  189.3 2.5 copy.48
  191.8 0.0 reduce-scatter.3.cloned.1.call-update
  191.8 0.0 reduce-scatter.5.cloned.1.call-start
  191.9 40.9 %reduce-scatter.3.cloned.1.call-done = bf16[2,512,128]{1,2,0:T(8,128)(2,1)} async-done(((bf16[16,512,128]{1,2,0:T(8,128)(2,1)}), bf16[2,512,128]{1,2,0:T(8,128)(2,1)}) %reduce-scatter.3.cloned.1.call-update) | async-done | bytes 262160 | tf_op jit(solution)/shard_map/reduce_scatter | solution.py:22
  232.8 0.0 reduce-scatter.5.cloned.1.call-update
  232.8 0.0 all-gather.4.cloned.1.call-start
  232.9 0.1 copy.51
  233.0 0.1 copy.45
  233.2 0.1 copy.49
  233.3 18.1 %reduce-scatter.5.cloned.1.call-done = bf16[1,512,128]{1,2,0:T(8,128)(2,1)} async-done(((bf16[2,512,128]{1,2,0:T(8,128)(2,1)}), bf16[1,512,128]{1,2,0:T(8,128)(2,1)}) %reduce-scatter.5.cloned.1.call-update) | async-done | bytes 131088 | tf_op jit(solution)/shard_map/reduce_scatter | solution.py:22
  251.4 1.8 fusion.14
  253.2 0.0 all-gather.4.cloned.1.call-update
  253.2 1.0 copy.52
  254.2 1.7 broadcast_in_dim.78
  256.0 7.5 %all-to-all-start.1 = ((bf16[16,512,128]{2,1,0:T(8,128)(2,1)}), bf16[16,512,128]{2,1,0:T(8,128)(2,1)S(1)}, u32[]{:S(2)}, u32[]{:S(2)}) async-start(bf16[16,512,128]{2,1,0:T(8,128)(2,1)} %broadcast_in_dim.78), calls=%async_computation.3 | async-start | bytes 4194304 | tf_op jit(solution)/shard_map/all_to_all | solution.py:38
  263.5 0.1 fusion.2
  263.6 0.1 iota_compare_fusion
  263.7 53.0 %all-gather.4.cloned.1.call-done = bf16[512,2048]{0,1:T(8,128)(2,1)} async-done(((bf16[512,128]{0,1:T(8,128)(2,1)}), bf16[512,2048]{0,1:T(8,128)(2,1)}) %all-gather.4.cloned.1.call-update) | async-done | bytes 2097168 | tf_op jit(solution)/shard_map/all_gather | solution.py:95
  316.7 19.3 %gather_fusion.1 = bf16[4096,512]{1,0:T(8,128)(2,1)} fusion(bf16[512,2048]{0,1:T(8,128)(2,1)} %all-gather.4.cloned.1.call-done, s32[4096]{0:T(1024)S(1)} %broadcast_clamp_fusion), kind=kCustom, calls=%fused_computation.1 | custom fusion | bytes 8404992 | tf_op jit(solution)/shard_map/jit(_take)/gather | solution.py:101
  336.0 5.2 %select_select_fusion = bf16[512,16,256]{0,2,1:T(8,128)(2,1)} fusion(bf16[512,16,256]{0,2,1:T(8,128)(2,1)} %bitcast.48, pred[16,256]{1,0:T(8,128)(4,1)S(1)} %get-tuple-element.35, pred[16,256]{1,0:T(8,128)(4,1)S(1)} %get-tuple-element.34), kind=kLoop, calls=%fused_computation.3 | loop fusion | flops 4194304 | bytes 8396800 | tf_op jit(solution)/shard_map/jit(_where)/select_n | solution.py:102
  341.2 11.2 %all-to-all-start.2 = ((bf16[512,16,256]{0,2,1:T(8,128)(2,1)}), bf16[512,16,256]{0,2,1:T(8,128)(2,1)}, u32[]{:S(2)}, u32[]{:S(2)}) async-start(bf16[512,16,256]{0,2,1:T(8,128)(2,1)} %select_select_fusion), calls=%async_computation.4 | async-start | bytes 8388608 | tf_op jit(solution)/shard_map/all_to_all | solution.py:104
  352.4 0.8 copy.54
  353.3 0.8 copy.56
  354.1 0.8 copy.55
  354.9 93.3 %all-to-all-done.2 = bf16[512,16,256]{0,2,1:T(8,128)(2,1)} async-done(((bf16[512,16,256]{0,2,1:T(8,128)(2,1)}), bf16[512,16,256]{0,2,1:T(8,128)(2,1)}, u32[]{:S(2)}, u32[]{:S(2)}) %all-to-all-start.2) | async-done | bytes 4194336 | tf_op jit(solution)/shard_map/all_to_all | solution.py:104
  448.3 6.4 %copy.53 = bf16[16,512,1,256]{3,1,0,2:T(8,128)(2,1)} copy(bf16[16,512,1,256]{1,3,0,2:T(8,128)(2,1)} %bitcast.18) | data formatting | bytes 8388608 | tf_op jit(solution)/shard_map/all_to_all | solution.py:104
  454.7 1.3 copy.60
  (9 shorter events, 0.1 us)
Async XLA Ops:
  7.2 148.3 %all-gather.6.cloned.1.call-start = ((), (), s32[]{:S(2)}) async-start(), calls=%async_computation.8 | async-start | bytes 17825792 | tf_op jit(solution)/shard_map/all_gather | solution.py:86
  7.9 224.9 %reduce-scatter.3.cloned.1.call-start = ((), (), s32[]{:S(2)}) async-start(), calls=%async_computation.5 | async-start | bytes 2359296 | tf_op jit(solution)/shard_map/reduce_scatter | solution.py:22
  189.3 43.6 %copy-start = (f32[512,128]{1,0:T(8,128)S(1)}, f32[512,128]{1,0:T(8,128)}, u32[]{:S(2)}) copy-start(f32[512,128]{1,0:T(8,128)} %param.9) | copy-start | bytes 786436
  189.3 43.7 %copy-start.1 = (f32[512,128]{1,0:T(8,128)S(1)}, f32[512,128]{1,0:T(8,128)}, u32[]{:S(2)}) copy-start(f32[512,128]{1,0:T(8,128)} %param.10) | copy-start | bytes 786436
  189.3 43.8 %copy-start.2 = (f32[512,128]{1,0:T(8,128)S(1)}, f32[512,128]{1,0:T(8,128)}, u32[]{:S(2)}) copy-start(f32[512,128]{1,0:T(8,128)} %param.11) | copy-start | bytes 786436
  191.8 59.6 %reduce-scatter.5.cloned.1.call-start = ((), (), s32[]{:S(2)}) async-start(), calls=%async_computation.6 | async-start | bytes 393216 | tf_op jit(solution)/shard_map/reduce_scatter | solution.py:22
  232.8 83.8 %all-gather.4.cloned.1.call-start = ((), (), s32[]{:S(2)}) async-start(), calls=%async_computation.7 | async-start | bytes 2228224 | tf_op jit(solution)/shard_map/all_gather | solution.py:95
  256.0 85.2 %all-to-all-start.1 = ((bf16[16,512,128]{2,1,0:T(8,128)(2,1)}), bf16[16,512,128]{2,1,0:T(8,128)(2,1)S(1)}, u32[]{:S(2)}, u32[]{:S(2)}) async-start(bf16[16,512,128]{2,1,0:T(8,128)(2,1)} %broadcast_in_dim.78), calls=%async_computation.3 | async-start | bytes 4194304 | tf_op jit(solution)/shard_map/all_to_all | solution.py:38
  341.2 107.1 %all-to-all-start.2 = ((bf16[512,16,256]{0,2,1:T(8,128)(2,1)}), bf16[512,16,256]{0,2,1:T(8,128)(2,1)}, u32[]{:S(2)}, u32[]{:S(2)}) async-start(bf16[512,16,256]{0,2,1:T(8,128)(2,1)} %select_select_fusion), calls=%async_computation.4 | async-start | bytes 8388608 | tf_op jit(solution)/shard_map/all_to_all | solution.py:104
Sparse Core Ops, SparseCore 0:
  10.7 144.7 all-gather.5
  192.0 40.7 reduce-scatter.2
  235.3 16.0 reduce-scatter.4
  254.5 62.0 all-gather.3
